TPU v7x, 32 devices: a whole 2x2x4 slice. The times are simulated.
32 devices in a mesh: grp: 2 (over y), node: 4 (over z), head: 4 (over x, core).
Axes of the slice: x: 2, y: 2, z: 4, core: 2. Of those that a mesh axis runs over, the one named last changes fastest.
Arguments:
- queries: bfloat16 [2048, 1024], P(('grp', 'node', 'head')), parts along dimension 0, may hold values from -8 to 8
- key_rows: bfloat16 [2048, 1024], P(('grp', 'node', 'head')), parts along dimension 0, may hold values from -8 to 8
- value_rows: bfloat16 [2048, 1024], P(('grp', 'node', 'head')), parts along dimension 0, may hold values from -6 to 6
- out_grads: bfloat16 [2048, 1024], P(('grp', 'node', 'head')), parts along dimension 0, may hold values from -6 to 6
- neighbours: int32 [16, 8], P('grp'), parts along dimension 0, may hold values from 0 to 7, as said below
Outputs:
- attended: bfloat16 [2048, 1024], P(('grp', 'node', 'head')), parts along dimension 0
- query_grad: bfloat16 [2048, 1024], P(('grp', 'node', 'head')), parts along dimension 0
- key_grad: bfloat16 [2048, 1024], P(('grp', 'node', 'head')), parts along dimension 0
- value_grad: bfloat16 [2048, 1024], P(('grp', 'node', 'head')), parts along dimension 0
There are 2 independent parts, one for each index of `grp`. A program takes and returns all parts, laid end to end along the dimension named above; each array names one. Nothing has to cross between parts.
Inputs may be any that keep to these rules, and one draw needn't show every extreme that they name: `neighbours`: the owner of patch p is p // 2. Every listed neighbour of a patch has an owner at distance at most 1 from the patch's owner. The patches of one owner together list exactly 1 distinct patches of each other owner within distance 1 that exists, and none of any other owner.
All inputs are finite; a program needn't handle non-finite values.
Results may differ from a plain program's by a relative error of at most 0.012.
Values may be sent and summed in bfloat16 or wider, within the bound.
A program may use at most 64 MiB of HBM per device.

v0:
```python
import functools
import math

import jax
import jax.numpy as jnp
from jax import lax
from jax.experimental import pallas as pl
from jax.experimental.pallas import tpu as pltpu
from jax.sharding import PartitionSpec as P

HEAD_DIM = 64
PATCH = 128
LANES = 128
MESH = pl.DeviceIdType.MESH
SCALE = HEAD_DIM ** (-0.5)
LOG2E = math.log2(math.e)
BF16 = jnp.bfloat16
F32 = jnp.float32


def dot(a, b):
    return jnp.dot(a, b, preferred_element_type=F32)


def kernel(
    heads, nodes, nbr_hbm, q_hbm, k_hbm, v_hbm, g_hbm,
    att_hbm, dq_hbm, dk_hbm, dv_hbm,
    nbr_ref, nbr_sem, pool, rows_in, halo_out, grad_out, grad_in, local_grad, result, turned, near,
    in_send, in_recv, in_local, halo_send, halo_recv,
    grad_send, grad_recv, out_send, out_recv, out_local,
):
    me = lax.axis_index("head")
    node = lax.axis_index("node")
    has_left, has_right = node > 0, node < nodes - 1
    chunks = pool.shape[1]
    part = q_hbm.shape[0]
    own = part * heads
    patches = own // PATCH
    listed = nbr_ref.shape[1]
    width = chunks * LANES
    peers = [lax.rem(me + d, heads) for d in range(1, heads)]
    sides = ((0, node - 1, has_left), (1, node + 1, has_right))

    lists = pltpu.make_async_copy(nbr_hbm, nbr_ref, nbr_sem)
    lists.start()
    barrier = pltpu.get_barrier_semaphore()
    for peer in peers:
        pl.semaphore_signal(barrier, inc=1, device_id={"head": peer}, device_id_type=MESH)
    for _, other, there in sides:
        @pl.when(there)
        def _():
            pl.semaphore_signal(barrier, inc=1, device_id={"node": other}, device_id_type=MESH)

    sources = (k_hbm, v_hbm, q_hbm, g_hbm)

    def landing(t, c):
        if t < 2:
            return pool.at[t, c, pl.ds(pl.multiple_of(PATCH + me * part, part), part), :]
        return rows_in.at[t - 2, c, pl.ds(pl.multiple_of(me * part, part), part), :]

    def in_copy(t, c, d):
        peer = peers[d]
        cols = pl.ds(pl.multiple_of(peer * width + c * LANES, LANES), LANES)
        return pltpu.make_async_remote_copy(
            src_ref=sources[t].at[:, cols], dst_ref=landing(t, c),
            send_sem=in_send.at[t, c, d], recv_sem=in_recv.at[t, c, d],
            device_id={"head": peer}, device_id_type=MESH,
        )

    def in_own(t, c):
        cols = pl.ds(pl.multiple_of(me * width + c * LANES, LANES), LANES)
        return pltpu.make_async_copy(sources[t].at[:, cols], landing(t, c), in_local.at[t, c])

    order = [(t, c) for ts in ((0, 1), (2, 3)) for c in range(chunks) for t in ts]
    for t, c in order:
        in_own(t, c).start()

    for side, _, there in sides:
        @pl.when(jnp.logical_not(there))
        def _():
            start = side * (PATCH + own)
            pool[:, :, start:start + PATCH, :] = jnp.zeros((2, chunks, PATCH, LANES), BF16)
            grad_in[:, :, side] = jnp.zeros((2, chunks, PATCH, LANES), BF16)

    pl.semaphore_wait(
        barrier, heads - 1 + has_left.astype(jnp.int32) + has_right.astype(jnp.int32)
    )
    for t, c in order:
        for d in range(heads - 1):
            in_copy(t, c, d).start()

    lists.wait()
    first = node * patches
    lane = lax.broadcasted_iota(jnp.int32, (1, own), 1)
    slot_counts = [jnp.zeros((1, own), F32) for _ in range(patches + 2)]
    for p in range(patches):
        counts = [jnp.int32(0)] * (patches + 2)
        counts[1 + p] = jnp.int32(1)
        for e in range(listed):
            value = nbr_ref[first + p, e]
            counts[0] += jnp.where(value < first, 1, 0)
            counts[-1] += jnp.where(value >= first + patches, 1, 0)
            for o in range(patches):
                counts[1 + o] += jnp.where(value == first + o, 1, 0)
        in_patch = (lane >= p * PATCH) & (lane < (p + 1) * PATCH)
        for s in range(patches + 2):
            slot_counts[s] = jnp.where(in_patch, counts[s].astype(F32), slot_counts[s])
    wanted = []
    for side, other, there in sides:
        start = jnp.clip(other, 0, nodes - 1) * patches
        pick = jnp.int32(0)
        for p in range(patches):
            for e in range(listed):
                value = nbr_ref[start + p, e]
                for o in range(1, patches):
                    pick = jnp.maximum(pick, jnp.where(value == first + o, o, 0))
        wanted.append(pick)

    def in_wait(t, c):
        in_own(t, c).wait()
        for d in range(heads - 1):
            in_copy(t, c, d).wait_recv()

    def halo_copy(t, c, side, other):
        start = (1 - side) * (PATCH + own)
        return pltpu.make_async_remote_copy(
            src_ref=halo_out.at[t, c, side], dst_ref=pool.at[t, c, pl.ds(start, PATCH), :],
            send_sem=halo_send.at[t, c, side], recv_sem=halo_recv.at[t, c, 1 - side],
            device_id={"node": other}, device_id_type=MESH,
        )

    def halo_arrived(t, c, side, other):
        start = side * (PATCH + own)
        return pltpu.make_async_remote_copy(
            src_ref=halo_out.at[t, c, side], dst_ref=pool.at[t, c, pl.ds(start, PATCH), :],
            send_sem=halo_send.at[t, c, side], recv_sem=halo_recv.at[t, c, side],
            device_id={"node": other}, device_id_type=MESH,
        )

    def grad_copy(t, c, side, other, arrived=False):
        far = side if arrived else 1 - side
        return pltpu.make_async_remote_copy(
            src_ref=grad_out.at[t, c, side], dst_ref=grad_in.at[t, c, far],
            send_sem=grad_send.at[t, c, side], recv_sem=grad_recv.at[t, c, far],
            device_id={"node": other}, device_id_type=MESH,
        )

    outs = (att_hbm, dq_hbm, dk_hbm, dv_hbm)

    def out_copy(t, c, d):
        peer = peers[d]
        cols = pl.ds(pl.multiple_of(me * width + c * LANES, LANES), LANES)
        return pltpu.make_async_remote_copy(
            src_ref=result.at[t, c, pl.ds(pl.multiple_of(peer * part, part), part), :],
            dst_ref=outs[t].at[:, cols],
            send_sem=out_send.at[t, c, d], recv_sem=out_recv.at[t, c, d],
            device_id={"head": peer}, device_id_type=MESH,
        )

    def out_own(t, c):
        cols = pl.ds(pl.multiple_of(me * width + c * LANES, LANES), LANES)
        return pltpu.make_async_copy(
            result.at[t, c, pl.ds(pl.multiple_of(me * part, part), part), :],
            outs[t].at[:, cols], out_local.at[t, c],
        )

    def out_start(t, c):
        for d in range(heads - 1):
            out_copy(t, c, d).start()
        out_own(t, c).start()

    for c in range(chunks):
        for t in range(2):
            in_wait(t, c)
            for side, other, there in sides:
                picked = pool[t, c, PATCH:2 * PATCH, :]
                for o in range(1, patches):
                    candidate = pool[t, c, (1 + o) * PATCH:(2 + o) * PATCH, :]
                    picked = jnp.where(wanted[side] == o, candidate, picked)
                halo_out[t, c, side] = picked

                @pl.when(there)
                def _():
                    halo_copy(t, c, side, other).start()

    group = LANES // HEAD_DIM

    def prepare(c):
        for t in (2, 3):
            in_wait(t, c)
            turned[t - 2, c] = rows_in[t - 2, c].T
        for h in range(group):
            head = (sub >= h * HEAD_DIM) & (sub < (h + 1) * HEAD_DIM)
            for t in range(2):
                part_t = jnp.where(head, turned[t, c], jnp.zeros((), BF16))
                block = dot(pool[t, c, PATCH:PATCH + own], part_t)
                near[t, c * group + h] = block * (SCALE * LOG2E) if t == 0 else block

    sub = lax.broadcasted_iota(jnp.int32, (LANES, own), 0)
    col = lax.broadcasted_iota(jnp.int32, (own, LANES), 1)
    for c in range(chunks):
        prepare(c)
        queries, grads = rows_in[0, c], rows_in[1, c]
        queries_t, grads_t = turned[0, c], turned[1, c]
        for side, other, there in sides:
            @pl.when(there)
            def _():
                for t in range(2):
                    halo_arrived(t, c, side, other).wait_recv()
        keys, values = pool[0, c], pool[1, c]
        keys_t, values_t = keys.T, values.T
        mixed_all, dq_all = [], []
        dk = dv = None
        for h in range(group):
            low, high = h * HEAD_DIM, (h + 1) * HEAD_DIM
            in_sub = (sub >= low) & (sub < high)
            in_col = (col >= low) & (col < high)
            zero = jnp.zeros((), BF16)
            u = c * group + h
            far_keys = jnp.concatenate([keys[:PATCH], keys[PATCH + own:]], 0)
            far_values = jnp.concatenate([values[:PATCH], values[PATCH + own:]], 0)
            far_scores = dot(far_keys, jnp.where(in_sub, queries_t, zero)) * (SCALE * LOG2E)
            far_probs = dot(far_values, jnp.where(in_sub, grads_t, zero))
            slots = [far_scores[:PATCH]]
            slots += [near[0, u, o * PATCH:(o + 1) * PATCH] for o in range(patches)]
            slots += [far_scores[PATCH:]]
            grad_probs = jnp.concatenate([far_probs[:PATCH], near[1, u], far_probs[PATCH:]], 0)
            tops = [
                jnp.where(n > 0, jnp.max(x, axis=0, keepdims=True), -jnp.inf)
                for n, x in zip(slot_counts, slots)
            ]
            top = functools.reduce(jnp.maximum, tops)
            exps = [
                jnp.exp2(x + jnp.where(n > 0, -top, -jnp.inf))
                for n, x in zip(slot_counts, slots)
            ]
            total = functools.reduce(
                jnp.add,
                [n * jnp.sum(x, axis=0, keepdims=True) for n, x in zip(slot_counts, exps)],
            )
            inverse = 1.0 / total
            probs = jnp.concatenate(
                [x * (n * inverse) for n, x in zip(slot_counts, exps)], 0
            )
            probs_low = probs.astype(BF16)
            mixed = dot(values_t[low:high], probs_low)
            row_dots = jnp.sum(
                grads_t[low:high].astype(F32) * mixed, axis=0, keepdims=True
            )
            grad_scores = (probs * (grad_probs - row_dots)).astype(BF16)
            mixed_all.append(mixed)
            dq_all.append(dot(keys_t[low:high], grad_scores) * SCALE)
            dk_h = dot(grad_scores, jnp.where(in_col, queries, zero))
            dv_h = dot(probs_low, jnp.where(in_col, grads, zero))
            dk = dk_h if dk is None else dk + dk_h
            dv = dv_h if dv is None else dv + dv_h
        for t, grad in enumerate((dk * SCALE, dv)):
            grad_out[t, c, 0] = grad[:PATCH].astype(BF16)
            grad_out[t, c, 1] = grad[PATCH + own:].astype(BF16)
            local_grad[t, c] = grad[PATCH:PATCH + own]
        for side, other, there in sides:
            @pl.when(there)
            def _():
                for t in range(2):
                    grad_copy(t, c, side, other).start()
        result[0, c] = jnp.concatenate(mixed_all, 0).T.astype(BF16)
        result[1, c] = jnp.concatenate(dq_all, 0).T.astype(BF16)
        out_start(0, c)
        out_start(1, c)

    for c in range(chunks):
        for side, other, there in sides:
            @pl.when(there)
            def _():
                for t in range(2):
                    grad_copy(t, c, side, other, arrived=True).wait_recv()
        for t in range(2):
            for o in range(patches):
                rows = slice(o * PATCH, (o + 1) * PATCH)
                total = local_grad[t, c, rows]
                for side in range(2):
                    total += jnp.where(wanted[side] == o, grad_in[t, c, side].astype(F32), 0.0)
                result[2 + t, c, rows] = total.astype(BF16)
            out_start(2 + t, c)

    for c in range(chunks):
        for t in range(4):
            out_own(t, c).wait()
            for d in range(heads - 1):
                in_copy(t, c, d).wait_send()
                out_copy(t, c, d).wait()
        for side, other, there in sides:
            @pl.when(there)
            def _():
                for t in range(2):
                    halo_copy(t, c, side, other).wait_send()
                    grad_copy(t, c, side, other).wait_send()


def write_out(*refs):
    sems = refs[8]
    copies = [pltpu.make_async_copy(refs[i], refs[4 + i], sems.at[i]) for i in range(4)]
    for copy in copies:
        copy.start()
    for copy in copies:
        copy.wait()


def solution(mesh):
    heads, nodes = mesh.shape["head"], mesh.shape["node"]

    def shards(queries, key_rows, value_rows, out_grads, neighbours):
        part, model = queries.shape
        own = part * heads
        chunks = model // heads // LANES
        pool_rows = own + 2 * PATCH
        any_spec = pl.BlockSpec(memory_space=pl.ANY)
        dma = pltpu.SemaphoreType.DMA
        landed = pl.pallas_call(
            functools.partial(kernel, heads, nodes),
            out_shape=[pltpu.VMEM((part, model), BF16)] * 4,
            in_specs=[any_spec] * 5,
            out_specs=[pl.BlockSpec(memory_space=pltpu.VMEM)] * 4,
            scratch_shapes=[
                pltpu.SMEM(neighbours.shape, jnp.int32),
                dma,
                pltpu.VMEM((2, chunks, pool_rows, LANES), BF16),
                pltpu.VMEM((2, chunks, own, LANES), BF16),
                pltpu.VMEM((2, chunks, 2, PATCH, LANES), BF16),
                pltpu.VMEM((2, chunks, 2, PATCH, LANES), BF16),
                pltpu.VMEM((2, chunks, 2, PATCH, LANES), BF16),
                pltpu.VMEM((2, chunks, own, LANES), F32),
                pltpu.VMEM((4, chunks, own, LANES), BF16),
                pltpu.VMEM((2, chunks, LANES, own), BF16),
                pltpu.VMEM((2, model // heads // HEAD_DIM, own, own), F32),
                dma((4, chunks, heads - 1)),
                dma((4, chunks, heads - 1)),
                dma((4, chunks)),
                dma((2, chunks, 2)),
                dma((2, chunks, 2)),
                dma((2, chunks, 2)),
                dma((2, chunks, 2)),
                dma((4, chunks, heads - 1)),
                dma((4, chunks, heads - 1)),
                dma((4, chunks)),
            ],
            compiler_params=pltpu.CompilerParams(collective_id=0, has_side_effects=True),
        )(neighbours, queries, key_rows, value_rows, out_grads)
        return pl.pallas_call(
            write_out,
            out_shape=[jax.ShapeDtypeStruct((part, model), BF16)] * 4,
            in_specs=[pl.BlockSpec(memory_space=pltpu.VMEM)] * 4,
            out_specs=[any_spec] * 4,
            scratch_shapes=[dma((4,))],
        )(*[pltpu.with_memory_space_constraint(x, pltpu.VMEM) for x in landed])

    rows = P(("grp", "node", "head"), None)
    return jax.shard_map(
        shards, mesh=mesh, in_specs=(rows, rows, rows, rows, P("grp", None)),
        out_specs=(rows,) * 4, check_vma=False,
    )
```

profile of v0, /device:TPU:0, one launch (start us, length us, event | category | flops | bytes accessed | tf_op | source)
XLA Modules:
  0.0 23.7 jit_solution(1198202567397337924)
XLA Ops:
  0.6 22.2 %shard_map.84 = (bf16[64,1024]{1,0:T(8,128)(2,1)S(1)}, bf16[64,1024]{1,0:T(8,128)(2,1)S(1)}, bf16[64,1024]{1,0:T(8,128)(2,1)S(1)}, bf16[64,1024]{1,0:T(8,128)(2,1)S(1)}) custom-call(s32[8,8]{1,0:T(8,128)} %nbr_hbm.1, bf16[64,1024]{1,0:T(8,128)(2,1)} %q_hbm.1, bf16[64,1024]{1,0:T(8,128)(2,1)} %k_hbm.1, bf16[64,1024]{1,0:T(8,128)(2,1)} %v_hbm.1, ...), custom_call_target="tpu_custom_call" | custom-call | tf_op jit(solution)/shard_map/pallas_call | solution.py:319
  22.8 0.8 %shard_map.85 = (bf16[64,1024]{1,0:T(8,128)(2,1)}, bf16[64,1024]{1,0:T(8,128)(2,1)}, bf16[64,1024]{1,0:T(8,128)(2,1)}, bf16[64,1024]{1,0:T(8,128)(2,1)}) custom-call(bf16[64,1024]{1,0:T(8,128)(2,1)S(1)} %get-tuple-element.8.refs_0_, bf16[64,1024]{1,0:T(8,128)(2,1)S(1)} %get-tuple-element.9.refs_1_, bf16[64,1024]{1,0:T(8,128)(2,1)S(1)} %get-tuple-element.10.refs_2_, ...), custom_call_target="tpu_custom_call" | custom-call | tf_op jit(solution)/shard_map/pallas_call | solution.py:349
where the time goes:
time: 23.8 us; the launch traced here: 23.7 us
  Pallas kernels  23 us (97%)
  between operations  0.64 us (3%)
    pallas_call x1, Pallas kernels, shards(): pl.pallas_call(functools.partial(kernel, heads, nodes), out_shape=[pltpu....  22.2 us
    pallas_call x1, Pallas kernels, shards(): pl.pallas_call(write_out, out_shape=[jax.ShapeDtypeStruct((part, model),...  0.82 us

commit v1 on v0

--- a/solution.py
+++ b/solution.py
@@ -26,8 +26,7 @@
     heads, nodes, nbr_hbm, q_hbm, k_hbm, v_hbm, g_hbm,
     att_hbm, dq_hbm, dk_hbm, dv_hbm,
     nbr_ref, nbr_sem, pool, rows_in, halo_out, grad_out, grad_in, local_grad, result, turned, near,
-    in_send, in_recv, in_local, halo_send, halo_recv,
-    grad_send, grad_recv, out_send, out_recv, out_local,
+    in_send, in_recv, halo_send, halo_recv, grad_send, grad_recv, out_send, out_recv,
 ):
     me = lax.axis_index("head")
     node = lax.axis_index("node")
@@ -63,13 +62,13 @@
         cols = pl.ds(pl.multiple_of(peer * width + c * LANES, LANES), LANES)
         return pltpu.make_async_remote_copy(
             src_ref=sources[t].at[:, cols], dst_ref=landing(t, c),
-            send_sem=in_send.at[t, c, d], recv_sem=in_recv.at[t, c, d],
+            send_sem=in_send, recv_sem=in_recv.at[t, c],
             device_id={"head": peer}, device_id_type=MESH,
         )
 
     def in_own(t, c):
         cols = pl.ds(pl.multiple_of(me * width + c * LANES, LANES), LANES)
-        return pltpu.make_async_copy(sources[t].at[:, cols], landing(t, c), in_local.at[t, c])
+        return pltpu.make_async_copy(sources[t].at[:, cols], landing(t, c), in_recv.at[t, c])
 
     order = [(t, c) for ts in ((0, 1), (2, 3)) for c in range(chunks) for t in ts]
     for t, c in order:
@@ -117,31 +116,33 @@
         wanted.append(pick)
 
     def in_wait(t, c):
-        in_own(t, c).wait()
-        for d in range(heads - 1):
-            in_copy(t, c, d).wait_recv()
+        if t < 2:
+            whole = pool.at[t, c, pl.ds(PATCH, own), :]
+        else:
+            whole = rows_in.at[t - 2, c]
+        pltpu.make_async_copy(whole, whole, in_recv.at[t, c]).wait()
 
     def halo_copy(t, c, side, other):
         start = (1 - side) * (PATCH + own)
         return pltpu.make_async_remote_copy(
-            src_ref=halo_out.at[t, c, side], dst_ref=pool.at[t, c, pl.ds(start, PATCH), :],
-            send_sem=halo_send.at[t, c, side], recv_sem=halo_recv.at[t, c, 1 - side],
+            src_ref=halo_out.at[side, t, c], dst_ref=pool.at[t, c, pl.ds(start, PATCH), :],
+            send_sem=halo_send.at[side], recv_sem=halo_recv.at[t, c, 1 - side],
             device_id={"node": other}, device_id_type=MESH,
         )
 
     def halo_arrived(t, c, side, other):
         start = side * (PATCH + own)
         return pltpu.make_async_remote_copy(
-            src_ref=halo_out.at[t, c, side], dst_ref=pool.at[t, c, pl.ds(start, PATCH), :],
-            send_sem=halo_send.at[t, c, side], recv_sem=halo_recv.at[t, c, side],
+            src_ref=halo_out.at[side, t, c], dst_ref=pool.at[t, c, pl.ds(start, PATCH), :],
+            send_sem=halo_send.at[side], recv_sem=halo_recv.at[t, c, side],
             device_id={"node": other}, device_id_type=MESH,
         )
 
     def grad_copy(t, c, side, other, arrived=False):
         far = side if arrived else 1 - side
         return pltpu.make_async_remote_copy(
-            src_ref=grad_out.at[t, c, side], dst_ref=grad_in.at[t, c, far],
-            send_sem=grad_send.at[t, c, side], recv_sem=grad_recv.at[t, c, far],
+            src_ref=grad_out.at[side, t, c], dst_ref=grad_in.at[t, c, far],
+            send_sem=grad_send.at[side], recv_sem=grad_recv.at[t, c, far],
             device_id={"node": other}, device_id_type=MESH,
         )
 
@@ -153,7 +154,7 @@
         return pltpu.make_async_remote_copy(
             src_ref=result.at[t, c, pl.ds(pl.multiple_of(peer * part, part), part), :],
             dst_ref=outs[t].at[:, cols],
-            send_sem=out_send.at[t, c, d], recv_sem=out_recv.at[t, c, d],
+            send_sem=out_send, recv_sem=out_recv,
             device_id={"head": peer}, device_id_type=MESH,
         )
 
@@ -161,7 +162,7 @@
         cols = pl.ds(pl.multiple_of(me * width + c * LANES, LANES), LANES)
         return pltpu.make_async_copy(
             result.at[t, c, pl.ds(pl.multiple_of(me * part, part), part), :],
-            outs[t].at[:, cols], out_local.at[t, c],
+            outs[t].at[:, cols], out_recv,
         )
 
     def out_start(t, c):
@@ -177,7 +178,7 @@
                 for o in range(1, patches):
                     candidate = pool[t, c, (1 + o) * PATCH:(2 + o) * PATCH, :]
                     picked = jnp.where(wanted[side] == o, candidate, picked)
-                halo_out[t, c, side] = picked
+                halo_out[side, t, c] = picked
 
                 @pl.when(there)
                 def _():
@@ -255,8 +256,8 @@
             dk = dk_h if dk is None else dk + dk_h
             dv = dv_h if dv is None else dv + dv_h
         for t, grad in enumerate((dk * SCALE, dv)):
-            grad_out[t, c, 0] = grad[:PATCH].astype(BF16)
-            grad_out[t, c, 1] = grad[PATCH + own:].astype(BF16)
+            grad_out[0, t, c] = grad[:PATCH].astype(BF16)
+            grad_out[1, t, c] = grad[PATCH + own:].astype(BF16)
             local_grad[t, c] = grad[PATCH:PATCH + own]
         for side, other, there in sides:
             @pl.when(there)
@@ -283,18 +284,16 @@
                 result[2 + t, c, rows] = total.astype(BF16)
             out_start(2 + t, c)
 
-    for c in range(chunks):
-        for t in range(4):
-            out_own(t, c).wait()
-            for d in range(heads - 1):
-                in_copy(t, c, d).wait_send()
-                out_copy(t, c, d).wait()
-        for side, other, there in sides:
-            @pl.when(there)
-            def _():
-                for t in range(2):
-                    halo_copy(t, c, side, other).wait_send()
-                    grad_copy(t, c, side, other).wait_send()
+    sent = result.at[:, :, pl.ds(0, own - part), :]
+    pltpu.make_async_copy(sent, sent, in_send).wait()
+    for side, other, there in sides:
+        @pl.when(there)
+        def _():
+            for out, sem in ((halo_out, halo_send), (grad_out, grad_send)):
+                block = out.at[side]
+                pltpu.make_async_copy(block, block, sem.at[side]).wait()
+    pltpu.make_async_copy(sent, sent, out_send).wait()
+    pltpu.make_async_copy(result, result, out_recv).wait()
 
 
 def write_out(*refs):
@@ -326,23 +325,21 @@
                 dma,
                 pltpu.VMEM((2, chunks, pool_rows, LANES), BF16),
                 pltpu.VMEM((2, chunks, own, LANES), BF16),
-                pltpu.VMEM((2, chunks, 2, PATCH, LANES), BF16),
-                pltpu.VMEM((2, chunks, 2, PATCH, LANES), BF16),
+                pltpu.VMEM((2, 2, chunks, PATCH, LANES), BF16),
+                pltpu.VMEM((2, 2, chunks, PATCH, LANES), BF16),
                 pltpu.VMEM((2, chunks, 2, PATCH, LANES), BF16),
                 pltpu.VMEM((2, chunks, own, LANES), F32),
                 pltpu.VMEM((4, chunks, own, LANES), BF16),
                 pltpu.VMEM((2, chunks, LANES, own), BF16),
                 pltpu.VMEM((2, model // heads // HEAD_DIM, own, own), F32),
-                dma((4, chunks, heads - 1)),
-                dma((4, chunks, heads - 1)),
+                dma,
                 dma((4, chunks)),
+                dma((2,)),
                 dma((2, chunks, 2)),
+                dma((2,)),
                 dma((2, chunks, 2)),
-                dma((2, chunks, 2)),
-                dma((2, chunks, 2)),
-                dma((4, chunks, heads - 1)),
-                dma((4, chunks, heads - 1)),
-                dma((4, chunks)),
+                dma,
+                dma,
             ],
             compiler_params=pltpu.CompilerParams(collective_id=0, has_side_effects=True),
         )(neighbours, queries, key_rows, value_rows, out_grads)

time: 23.8 us -> 22.8 us (0.958)
  Pallas kernels: 23 us -> 22 us
    pallas_call x1, Pallas kernels: 22.2 us -> 21.2 us  [shards(): pl.pallas_call(functools.partial(kernel, heads, nodes), out_shape=[pltpu....]
where the time goes in v1:
time: 22.8 us; the launch traced here: 22.6 us
  Pallas kernels  22 us (96%)
  between operations  0.64 us (3%)
    pallas_call x1, Pallas kernels, shards(): pl.pallas_call(functools.partial(kernel, heads, nodes), out_shape=[pltpu....  21.2 us
    pallas_call x1, Pallas kernels, shards(): pl.pallas_call(write_out, out_shape=[jax.ShapeDtypeStruct((part, model),...  0.82 us

profile of v1, /device:TPU:0, one launch (start us, length us, event | category | flops | bytes accessed | tf_op | source)
XLA Modules:
  0.0 22.6 jit_solution(16224210193791736667)
XLA Ops:
  0.6 21.2 %shard_map.84 = (bf16[64,1024]{1,0:T(8,128)(2,1)S(1)}, bf16[64,1024]{1,0:T(8,128)(2,1)S(1)}, bf16[64,1024]{1,0:T(8,128)(2,1)S(1)}, bf16[64,1024]{1,0:T(8,128)(2,1)S(1)}) custom-call(s32[8,8]{1,0:T(8,128)} %nbr_hbm.1, bf16[64,1024]{1,0:T(8,128)(2,1)} %q_hbm.1, bf16[64,1024]{1,0:T(8,128)(2,1)} %k_hbm.1, bf16[64,1024]{1,0:T(8,128)(2,1)} %v_hbm.1, ...), custom_call_target="tpu_custom_call" | custom-call | tf_op jit(solution)/shard_map/pallas_call | solution.py:318
  21.8 0.8 %shard_map.85 = (bf16[64,1024]{1,0:T(8,128)(2,1)}, bf16[64,1024]{1,0:T(8,128)(2,1)}, bf16[64,1024]{1,0:T(8,128)(2,1)}, bf16[64,1024]{1,0:T(8,128)(2,1)}) custom-call(bf16[64,1024]{1,0:T(8,128)(2,1)S(1)} %get-tuple-element.8.refs_0_, bf16[64,1024]{1,0:T(8,128)(2,1)S(1)} %get-tuple-element.9.refs_1_, bf16[64,1024]{1,0:T(8,128)(2,1)S(1)} %get-tuple-element.10.refs_2_, ...), custom_call_target="tpu_custom_call" | custom-call | tf_op jit(solution)/shard_map/pallas_call | solution.py:346

commit v2 on v1

--- a/solution.py
+++ b/solution.py
@@ -25,7 +25,7 @@
 def kernel(
     heads, nodes, nbr_hbm, q_hbm, k_hbm, v_hbm, g_hbm,
     att_hbm, dq_hbm, dk_hbm, dv_hbm,
-    nbr_ref, nbr_sem, pool, rows_in, halo_out, grad_out, grad_in, local_grad, result, turned, near,
+    nbr_ref, nbr_sem, pool, rows_in, halo_out, grad_out, grad_in, result, turned, near, kept,
     in_send, in_recv, halo_send, halo_recv, grad_send, grad_recv, out_send, out_recv,
 ):
     me = lax.axis_index("head")
@@ -170,7 +170,7 @@
             out_copy(t, c, d).start()
         out_own(t, c).start()
 
-    for c in range(chunks):
+    def forward_halo(c):
         for t in range(2):
             in_wait(t, c)
             for side, other, there in sides:
@@ -185,104 +185,152 @@
                     halo_copy(t, c, side, other).start()
 
     group = LANES // HEAD_DIM
+    sub = lax.broadcasted_iota(jnp.int32, (LANES, own), 0)
+    col = lax.broadcasted_iota(jnp.int32, (own, LANES), 1)
+    zero = jnp.zeros((), BF16)
+    span = [(h * HEAD_DIM, (h + 1) * HEAD_DIM) for h in range(group)]
+    sub_heads = [(sub >= low) & (sub < high) for low, high in span]
+    col_heads = [(col >= low) & (col < high) for low, high in span]
+    near_counts = slot_counts[1:-1]
+    far_counts = (slot_counts[0], slot_counts[-1])
+
+    def shifted(n, x, top):
+        return jnp.exp2(x + jnp.where(n > 0, -top, -jnp.inf))
+
+    def highest(n, x):
+        return jnp.where(n > 0, jnp.max(x, axis=0, keepdims=True), -jnp.inf)
+
+    def rows_of(x, o):
+        return x[o * PATCH:(o + 1) * PATCH]
 
     def prepare(c):
+        stats = []
         for t in (2, 3):
             in_wait(t, c)
             turned[t - 2, c] = rows_in[t - 2, c].T
+        for t in range(2):
+            turned[2 + t, c] = pool[t, c, PATCH:PATCH + own].T
         for h in range(group):
-            head = (sub >= h * HEAD_DIM) & (sub < (h + 1) * HEAD_DIM)
-            for t in range(2):
-                part_t = jnp.where(head, turned[t, c], jnp.zeros((), BF16))
-                block = dot(pool[t, c, PATCH:PATCH + own], part_t)
-                near[t, c * group + h] = block * (SCALE * LOG2E) if t == 0 else block
-
-    sub = lax.broadcasted_iota(jnp.int32, (LANES, own), 0)
-    col = lax.broadcasted_iota(jnp.int32, (own, LANES), 1)
-    for c in range(chunks):
-        prepare(c)
-        queries, grads = rows_in[0, c], rows_in[1, c]
-        queries_t, grads_t = turned[0, c], turned[1, c]
+            u = c * group + h
+            scores = dot(pool[0, c, PATCH:PATCH + own], jnp.where(sub_heads[h], turned[0, c], zero))
+            scores = scores * (SCALE * LOG2E)
+            top = functools.reduce(
+                jnp.maximum, [highest(n, rows_of(scores, o)) for o, n in enumerate(near_counts)]
+            )
+            total = jnp.zeros((1, own), F32)
+            for o, n in enumerate(near_counts):
+                x = shifted(n, rows_of(scores, o), top)
+                near[0, u, o * PATCH:(o + 1) * PATCH] = x
+                total += n * jnp.sum(x, axis=0, keepdims=True)
+            stats.append((top, total))
+            near[1, u] = dot(
+                pool[1, c, PATCH:PATCH + own], jnp.where(sub_heads[h], turned[1, c], zero)
+            )
+        return stats
+
+    def far_rows(t, c):
+        return jnp.concatenate([pool[t, c, :PATCH], pool[t, c, PATCH + own:]], 0)
+
+    def halo_wait(t, c):
         for side, other, there in sides:
             @pl.when(there)
             def _():
-                for t in range(2):
-                    halo_arrived(t, c, side, other).wait_recv()
-        keys, values = pool[0, c], pool[1, c]
-        keys_t, values_t = keys.T, values.T
-        mixed_all, dq_all = [], []
-        dk = dv = None
+                halo_arrived(t, c, side, other).wait_recv()
+
+    def send_grad(t, c, grad):
+        for side, other, there in sides:
+            grad_out[side, t, c] = rows_of(grad, side).astype(BF16)
+
+            @pl.when(there)
+            def _():
+                grad_copy(t, c, side, other).start()
+
+    def attend(c, stats):
+        grads_t = turned[1, c]
+        halo_wait(0, c)
+        far_keys = far_rows(0, c)
+        probs = []
         for h in range(group):
-            low, high = h * HEAD_DIM, (h + 1) * HEAD_DIM
-            in_sub = (sub >= low) & (sub < high)
-            in_col = (col >= low) & (col < high)
-            zero = jnp.zeros((), BF16)
             u = c * group + h
-            far_keys = jnp.concatenate([keys[:PATCH], keys[PATCH + own:]], 0)
-            far_values = jnp.concatenate([values[:PATCH], values[PATCH + own:]], 0)
-            far_scores = dot(far_keys, jnp.where(in_sub, queries_t, zero)) * (SCALE * LOG2E)
-            far_probs = dot(far_values, jnp.where(in_sub, grads_t, zero))
-            slots = [far_scores[:PATCH]]
-            slots += [near[0, u, o * PATCH:(o + 1) * PATCH] for o in range(patches)]
-            slots += [far_scores[PATCH:]]
-            grad_probs = jnp.concatenate([far_probs[:PATCH], near[1, u], far_probs[PATCH:]], 0)
-            tops = [
-                jnp.where(n > 0, jnp.max(x, axis=0, keepdims=True), -jnp.inf)
-                for n, x in zip(slot_counts, slots)
-            ]
-            top = functools.reduce(jnp.maximum, tops)
-            exps = [
-                jnp.exp2(x + jnp.where(n > 0, -top, -jnp.inf))
-                for n, x in zip(slot_counts, slots)
-            ]
+            scores = dot(far_keys, jnp.where(sub_heads[h], turned[0, c], zero)) * (SCALE * LOG2E)
+            near_top, near_total = stats[h]
+            top = functools.reduce(
+                jnp.maximum, [highest(n, rows_of(scores, i)) for i, n in enumerate(far_counts)], near_top
+            )
+            exps = [shifted(n, rows_of(scores, i), top) for i, n in enumerate(far_counts)]
+            alpha = jnp.exp2(near_top - top)
+            total = near_total * alpha
+            for n, x in zip(far_counts, exps):
+                total += n * jnp.sum(x, axis=0, keepdims=True)
+            inverse = 1.0 / total
+            far = jnp.concatenate([x * (n * inverse) for n, x in zip(far_counts, exps)], 0)
+            factor = alpha * inverse
+            close = jnp.concatenate(
+                [near[0, u, o * PATCH:(o + 1) * PATCH] * (n * factor) for o, n in enumerate(near_counts)], 0
+            )
+            kept[0, u] = close.astype(BF16)
+            probs.append((close, far, far.astype(BF16)))
+        halo_wait(1, c)
+        far_values = far_rows(1, c)
+        far_values_t, far_keys_t = far_values.T, far_keys.T
+        mixed = [
+            dot(turned[3, c, low:high], kept[0, c * group + h]) + dot(far_values_t[low:high], probs[h][2])
+            for h, (low, high) in enumerate(span)
+        ]
+        result[0, c] = jnp.concatenate(mixed, 0).T.astype(BF16)
+        out_start(0, c)
+        dv = functools.reduce(
+            jnp.add,
+            [dot(probs[h][2], jnp.where(col_heads[h], rows_in[1, c], zero)) for h in range(group)],
+        )
+        send_grad(1, c, dv)
+        dq_all, dk = [], None
+        for h, (low, high) in enumerate(span):
+            u = c * group + h
+            close, far, _ = probs[h]
+            row_dots = jnp.sum(grads_t[low:high].astype(F32) * mixed[h], axis=0, keepdims=True)
+            grad_far = dot(far_values, jnp.where(sub_heads[h], grads_t, zero))
+            far_scores = (far * (grad_far - row_dots)).astype(BF16)
+            close_scores = (close * (near[1, u] - row_dots)).astype(BF16)
+            kept[1, u] = close_scores
+            dk_h = dot(far_scores, jnp.where(col_heads[h], rows_in[0, c], zero))
+            dk = dk_h if dk is None else dk + dk_h
+            dq_all.append(
+                (dot(turned[2, c, low:high], close_scores) + dot(far_keys_t[low:high], far_scores)) * SCALE
+            )
+        send_grad(0, c, dk * SCALE)
+        result[1, c] = jnp.concatenate(dq_all, 0).T.astype(BF16)
+        out_start(1, c)
+
+    def finish(c):
+        for t in (1, 0):
             total = functools.reduce(
                 jnp.add,
-                [n * jnp.sum(x, axis=0, keepdims=True) for n, x in zip(slot_counts, exps)],
-            )
-            inverse = 1.0 / total
-            probs = jnp.concatenate(
-                [x * (n * inverse) for n, x in zip(slot_counts, exps)], 0
-            )
-            probs_low = probs.astype(BF16)
-            mixed = dot(values_t[low:high], probs_low)
-            row_dots = jnp.sum(
-                grads_t[low:high].astype(F32) * mixed, axis=0, keepdims=True
-            )
-            grad_scores = (probs * (grad_probs - row_dots)).astype(BF16)
-            mixed_all.append(mixed)
-            dq_all.append(dot(keys_t[low:high], grad_scores) * SCALE)
-            dk_h = dot(grad_scores, jnp.where(in_col, queries, zero))
-            dv_h = dot(probs_low, jnp.where(in_col, grads, zero))
-            dk = dk_h if dk is None else dk + dk_h
-            dv = dv_h if dv is None else dv + dv_h
-        for t, grad in enumerate((dk * SCALE, dv)):
-            grad_out[0, t, c] = grad[:PATCH].astype(BF16)
-            grad_out[1, t, c] = grad[PATCH + own:].astype(BF16)
-            local_grad[t, c] = grad[PATCH:PATCH + own]
-        for side, other, there in sides:
-            @pl.when(there)
-            def _():
-                for t in range(2):
-                    grad_copy(t, c, side, other).start()
-        result[0, c] = jnp.concatenate(mixed_all, 0).T.astype(BF16)
-        result[1, c] = jnp.concatenate(dq_all, 0).T.astype(BF16)
-        out_start(0, c)
-        out_start(1, c)
-
-    for c in range(chunks):
-        for side, other, there in sides:
-            @pl.when(there)
-            def _():
-                for t in range(2):
+                [
+                    dot(kept[1 - t, c * group + h], jnp.where(col_heads[h], rows_in[t, c], zero))
+                    for h in range(group)
+                ],
+            )
+            if t == 0:
+                total = total * SCALE
+            for side, other, there in sides:
+                @pl.when(there)
+                def _():
                     grad_copy(t, c, side, other, arrived=True).wait_recv()
-        for t in range(2):
             for o in range(patches):
                 rows = slice(o * PATCH, (o + 1) * PATCH)
-                total = local_grad[t, c, rows]
+                block = total[rows]
                 for side in range(2):
-                    total += jnp.where(wanted[side] == o, grad_in[t, c, side].astype(F32), 0.0)
-                result[2 + t, c, rows] = total.astype(BF16)
+                    block += jnp.where(wanted[side] == o, grad_in[t, c, side].astype(F32), 0.0)
+                result[2 + t, c, rows] = block.astype(BF16)
             out_start(2 + t, c)
+
+    for c in range(chunks):
+        forward_halo(c)
+    for c in range(chunks):
+        attend(c, prepare(c))
+    for c in range(chunks):
+        finish(c)
 
     sent = result.at[:, :, pl.ds(0, own - part), :]
     pltpu.make_async_copy(sent, sent, in_send).wait()
@@ -328,10 +376,10 @@
                 pltpu.VMEM((2, 2, chunks, PATCH, LANES), BF16),
                 pltpu.VMEM((2, 2, chunks, PATCH, LANES), BF16),
                 pltpu.VMEM((2, chunks, 2, PATCH, LANES), BF16),
-                pltpu.VMEM((2, chunks, own, LANES), F32),
                 pltpu.VMEM((4, chunks, own, LANES), BF16),
-                pltpu.VMEM((2, chunks, LANES, own), BF16),
+                pltpu.VMEM((4, chunks, LANES, own), BF16),
                 pltpu.VMEM((2, model // heads // HEAD_DIM, own, own), F32),
+                pltpu.VMEM((2, model // heads // HEAD_DIM, own, own), BF16),
                 dma,
                 dma((4, chunks)),
                 dma((2,)),

time: 22.8 us -> 22 us (0.965)
  Pallas kernels: 22 us -> 21.2 us
    pallas_call x1, Pallas kernels: 21.2 us -> 20.4 us  [shards(): pl.pallas_call(functools.partial(kernel, heads, nodes), out_shape=[pltpu....]
where the time goes in v2:
time: 22 us; the launch traced here: 21.8 us
  Pallas kernels  21.2 us (96%)
  between operations  0.64 us (3%)
    pallas_call x1, Pallas kernels, shards(): pl.pallas_call(functools.partial(kernel, heads, nodes), out_shape=[pltpu....  20.4 us
    pallas_call x1, Pallas kernels, shards(): pl.pallas_call(write_out, out_shape=[jax.ShapeDtypeStruct((part, model),...  0.82 us

profile of v2, /device:TPU:0, one launch (start us, length us, event | category | flops | bytes accessed | tf_op | source)
XLA Modules:
  0.0 21.8 jit_solution(13240472221340421424)
XLA Ops:
  0.6 20.4 %shard_map.84 = (bf16[64,1024]{1,0:T(8,128)(2,1)S(1)}, bf16[64,1024]{1,0:T(8,128)(2,1)S(1)}, bf16[64,1024]{1,0:T(8,128)(2,1)S(1)}, bf16[64,1024]{1,0:T(8,128)(2,1)S(1)}) custom-call(s32[8,8]{1,0:T(8,128)} %nbr_hbm.1, bf16[64,1024]{1,0:T(8,128)(2,1)} %q_hbm.1, bf16[64,1024]{1,0:T(8,128)(2,1)} %k_hbm.1, bf16[64,1024]{1,0:T(8,128)(2,1)} %v_hbm.1, ...), custom_call_target="tpu_custom_call" | custom-call | tf_op jit(solution)/shard_map/pallas_call | solution.py:366
  21.0 0.8 %shard_map.85 = (bf16[64,1024]{1,0:T(8,128)(2,1)}, bf16[64,1024]{1,0:T(8,128)(2,1)}, bf16[64,1024]{1,0:T(8,128)(2,1)}, bf16[64,1024]{1,0:T(8,128)(2,1)}) custom-call(bf16[64,1024]{1,0:T(8,128)(2,1)S(1)} %get-tuple-element.8.refs_0_, bf16[64,1024]{1,0:T(8,128)(2,1)S(1)} %get-tuple-element.9.refs_1_, bf16[64,1024]{1,0:T(8,128)(2,1)S(1)} %get-tuple-element.10.refs_2_, ...), custom_call_target="tpu_custom_call" | custom-call | tf_op jit(solution)/shard_map/pallas_call | solution.py:394

commit v3 on v2

--- a/solution.py
+++ b/solution.py
@@ -26,7 +26,7 @@
     heads, nodes, nbr_hbm, q_hbm, k_hbm, v_hbm, g_hbm,
     att_hbm, dq_hbm, dk_hbm, dv_hbm,
     nbr_ref, nbr_sem, pool, rows_in, halo_out, grad_out, grad_in, result, turned, near, kept,
-    in_send, in_recv, halo_send, halo_recv, grad_send, grad_recv, out_send, out_recv,
+    ready, in_send, in_recv, halo_send, halo_recv, grad_send, grad_recv, out_send, out_recv,
 ):
     me = lax.axis_index("head")
     node = lax.axis_index("node")
@@ -45,10 +45,10 @@
     barrier = pltpu.get_barrier_semaphore()
     for peer in peers:
         pl.semaphore_signal(barrier, inc=1, device_id={"head": peer}, device_id_type=MESH)
-    for _, other, there in sides:
-        @pl.when(there)
-        def _():
-            pl.semaphore_signal(barrier, inc=1, device_id={"node": other}, device_id_type=MESH)
+
+    @pl.when(has_right)
+    def _():
+        pl.semaphore_signal(barrier, inc=1, device_id={"node": node + 1}, device_id_type=MESH)
 
     sources = (k_hbm, v_hbm, q_hbm, g_hbm)
 
@@ -71,8 +71,6 @@
         return pltpu.make_async_copy(sources[t].at[:, cols], landing(t, c), in_recv.at[t, c])
 
     order = [(t, c) for ts in ((0, 1), (2, 3)) for c in range(chunks) for t in ts]
-    for t, c in order:
-        in_own(t, c).start()
 
     for side, _, there in sides:
         @pl.when(jnp.logical_not(there))
@@ -81,12 +79,17 @@
             pool[:, :, start:start + PATCH, :] = jnp.zeros((2, chunks, PATCH, LANES), BF16)
             grad_in[:, :, side] = jnp.zeros((2, chunks, PATCH, LANES), BF16)
 
-    pl.semaphore_wait(
-        barrier, heads - 1 + has_left.astype(jnp.int32) + has_right.astype(jnp.int32)
-    )
+    pl.semaphore_wait(barrier, heads - 1 + has_left.astype(jnp.int32))
+
+    @pl.when(has_left)
+    def _():
+        pl.semaphore_signal(ready, inc=1, device_id={"node": node - 1}, device_id_type=MESH)
+
     for t, c in order:
         for d in range(heads - 1):
             in_copy(t, c, d).start()
+    for t, c in order:
+        in_own(t, c).start()
 
     lists.wait()
     first = node * patches
@@ -205,11 +208,8 @@
 
     def prepare(c):
         stats = []
-        for t in (2, 3):
-            in_wait(t, c)
-            turned[t - 2, c] = rows_in[t - 2, c].T
-        for t in range(2):
-            turned[2 + t, c] = pool[t, c, PATCH:PATCH + own].T
+        in_wait(2, c)
+        turned[0, c] = rows_in[0, c].T
         for h in range(group):
             u = c * group + h
             scores = dot(pool[0, c, PATCH:PATCH + own], jnp.where(sub_heads[h], turned[0, c], zero))
@@ -220,12 +220,9 @@
             total = jnp.zeros((1, own), F32)
             for o, n in enumerate(near_counts):
                 x = shifted(n, rows_of(scores, o), top)
-                near[0, u, o * PATCH:(o + 1) * PATCH] = x
+                near[u, o * PATCH:(o + 1) * PATCH] = x
                 total += n * jnp.sum(x, axis=0, keepdims=True)
             stats.append((top, total))
-            near[1, u] = dot(
-                pool[1, c, PATCH:PATCH + own], jnp.where(sub_heads[h], turned[1, c], zero)
-            )
         return stats
 
     def far_rows(t, c):
@@ -246,7 +243,6 @@
                 grad_copy(t, c, side, other).start()
 
     def attend(c, stats):
-        grads_t = turned[1, c]
         halo_wait(0, c)
         far_keys = far_rows(0, c)
         probs = []
@@ -266,24 +262,28 @@
             far = jnp.concatenate([x * (n * inverse) for n, x in zip(far_counts, exps)], 0)
             factor = alpha * inverse
             close = jnp.concatenate(
-                [near[0, u, o * PATCH:(o + 1) * PATCH] * (n * factor) for o, n in enumerate(near_counts)], 0
+                [near[u, o * PATCH:(o + 1) * PATCH] * (n * factor) for o, n in enumerate(near_counts)], 0
             )
             kept[0, u] = close.astype(BF16)
             probs.append((close, far, far.astype(BF16)))
         halo_wait(1, c)
         far_values = far_rows(1, c)
-        far_values_t, far_keys_t = far_values.T, far_keys.T
+        far_values_t = far_values.T
         mixed = [
             dot(turned[3, c, low:high], kept[0, c * group + h]) + dot(far_values_t[low:high], probs[h][2])
             for h, (low, high) in enumerate(span)
         ]
         result[0, c] = jnp.concatenate(mixed, 0).T.astype(BF16)
         out_start(0, c)
+        in_wait(3, c)
+        turned[1, c] = rows_in[1, c].T
+        grads_t = turned[1, c]
         dv = functools.reduce(
             jnp.add,
             [dot(probs[h][2], jnp.where(col_heads[h], rows_in[1, c], zero)) for h in range(group)],
         )
         send_grad(1, c, dv)
+        far_keys_t = far_keys.T
         dq_all, dk = [], None
         for h, (low, high) in enumerate(span):
             u = c * group + h
@@ -291,7 +291,8 @@
             row_dots = jnp.sum(grads_t[low:high].astype(F32) * mixed[h], axis=0, keepdims=True)
             grad_far = dot(far_values, jnp.where(sub_heads[h], grads_t, zero))
             far_scores = (far * (grad_far - row_dots)).astype(BF16)
-            close_scores = (close * (near[1, u] - row_dots)).astype(BF16)
+            grad_near = dot(pool[1, c, PATCH:PATCH + own], jnp.where(sub_heads[h], grads_t, zero))
+            close_scores = (close * (grad_near - row_dots)).astype(BF16)
             kept[1, u] = close_scores
             dk_h = dot(far_scores, jnp.where(col_heads[h], rows_in[0, c], zero))
             dk = dk_h if dk is None else dk + dk_h
@@ -325,8 +326,15 @@
                 result[2 + t, c, rows] = block.astype(BF16)
             out_start(2 + t, c)
 
+    @pl.when(has_right)
+    def _():
+        pl.semaphore_wait(ready, 1)
+
     for c in range(chunks):
         forward_halo(c)
+    for c in range(chunks):
+        for t in range(2):
+            turned[2 + t, c] = pool[t, c, PATCH:PATCH + own].T
     for c in range(chunks):
         attend(c, prepare(c))
     for c in range(chunks):
@@ -378,8 +386,9 @@
                 pltpu.VMEM((2, chunks, 2, PATCH, LANES), BF16),
                 pltpu.VMEM((4, chunks, own, LANES), BF16),
                 pltpu.VMEM((4, chunks, LANES, own), BF16),
-                pltpu.VMEM((2, model // heads // HEAD_DIM, own, own), F32),
+                pltpu.VMEM((model // heads // HEAD_DIM, own, own), F32),
                 pltpu.VMEM((2, model // heads // HEAD_DIM, own, own), BF16),
+                pltpu.SemaphoreType.REGULAR,
                 dma,
                 dma((4, chunks)),
                 dma((2,)),

time: 22 us -> 21.5 us (0.977)
  Pallas kernels: 21.2 us -> 20.7 us
    pallas_call x1, Pallas kernels: 20.4 us -> 19.9 us  [shards(): pl.pallas_call(functools.partial(kernel, heads, nodes), out_shape=[pltpu....]
where the time goes in v3:
time: 21.5 us; the launch traced here: 21.4 us
  Pallas kernels  20.7 us (96%)
  between operations  0.64 us (3%)
    pallas_call x1, Pallas kernels, shards(): pl.pallas_call(functools.partial(kernel, heads, nodes), out_shape=[pltpu....  19.9 us
    pallas_call x1, Pallas kernels, shards(): pl.pallas_call(write_out, out_shape=[jax.ShapeDtypeStruct((part, model),...  0.82 us

profile of v3, /device:TPU:0, one launch (start us, length us, event | category | flops | bytes accessed | tf_op | source)
XLA Modules:
  0.0 21.4 jit_solution(4022786164817445521)
XLA Ops:
  0.6 19.9 %shard_map.84 = (bf16[64,1024]{1,0:T(8,128)(2,1)S(1)}, bf16[64,1024]{1,0:T(8,128)(2,1)S(1)}, bf16[64,1024]{1,0:T(8,128)(2,1)S(1)}, bf16[64,1024]{1,0:T(8,128)(2,1)S(1)}) custom-call(s32[8,8]{1,0:T(8,128)} %nbr_hbm.1, bf16[64,1024]{1,0:T(8,128)(2,1)} %q_hbm.1, bf16[64,1024]{1,0:T(8,128)(2,1)} %k_hbm.1, bf16[64,1024]{1,0:T(8,128)(2,1)} %v_hbm.1, ...), custom_call_target="tpu_custom_call" | custom-call | tf_op jit(solution)/shard_map/pallas_call | solution.py:374
  20.5 0.8 %shard_map.85 = (bf16[64,1024]{1,0:T(8,128)(2,1)}, bf16[64,1024]{1,0:T(8,128)(2,1)}, bf16[64,1024]{1,0:T(8,128)(2,1)}, bf16[64,1024]{1,0:T(8,128)(2,1)}) custom-call(bf16[64,1024]{1,0:T(8,128)(2,1)S(1)} %get-tuple-element.8.refs_0_, bf16[64,1024]{1,0:T(8,128)(2,1)S(1)} %get-tuple-element.9.refs_1_, bf16[64,1024]{1,0:T(8,128)(2,1)S(1)} %get-tuple-element.10.refs_2_, ...), custom_call_target="tpu_custom_call" | custom-call | tf_op jit(solution)/shard_map/pallas_call | solution.py:403

commit v4 on v3

--- a/solution.py
+++ b/solution.py
@@ -24,7 +24,7 @@
 
 def kernel(
     heads, nodes, nbr_hbm, q_hbm, k_hbm, v_hbm, g_hbm,
-    att_hbm, dq_hbm, dk_hbm, dv_hbm,
+    landed,
     nbr_ref, nbr_sem, pool, rows_in, halo_out, grad_out, grad_in, result, turned, near, kept,
     ready, in_send, in_recv, halo_send, halo_recv, grad_send, grad_recv, out_send, out_recv,
 ):
@@ -72,24 +72,24 @@
 
     order = [(t, c) for ts in ((0, 1), (2, 3)) for c in range(chunks) for t in ts]
 
+    pl.semaphore_wait(barrier, heads - 1 + has_left.astype(jnp.int32))
+
+    @pl.when(has_left)
+    def _():
+        pl.semaphore_signal(ready, inc=1, device_id={"node": node - 1}, device_id_type=MESH)
+
+    for t, c in order:
+        for d in range(heads - 1):
+            in_copy(t, c, d).start()
+    for t, c in order:
+        in_own(t, c).start()
+
     for side, _, there in sides:
         @pl.when(jnp.logical_not(there))
         def _():
             start = side * (PATCH + own)
             pool[:, :, start:start + PATCH, :] = jnp.zeros((2, chunks, PATCH, LANES), BF16)
             grad_in[:, :, side] = jnp.zeros((2, chunks, PATCH, LANES), BF16)
-
-    pl.semaphore_wait(barrier, heads - 1 + has_left.astype(jnp.int32))
-
-    @pl.when(has_left)
-    def _():
-        pl.semaphore_signal(ready, inc=1, device_id={"node": node - 1}, device_id_type=MESH)
-
-    for t, c in order:
-        for d in range(heads - 1):
-            in_copy(t, c, d).start()
-    for t, c in order:
-        in_own(t, c).start()
 
     lists.wait()
     first = node * patches
@@ -129,27 +129,27 @@
         start = (1 - side) * (PATCH + own)
         return pltpu.make_async_remote_copy(
             src_ref=halo_out.at[side, t, c], dst_ref=pool.at[t, c, pl.ds(start, PATCH), :],
-            send_sem=halo_send.at[side], recv_sem=halo_recv.at[t, c, 1 - side],
+            send_sem=halo_send, recv_sem=halo_recv.at[t, c],
             device_id={"node": other}, device_id_type=MESH,
         )
 
-    def halo_arrived(t, c, side, other):
-        start = side * (PATCH + own)
+    def sides_wait(two, one, sem):
+        @pl.when(has_left & has_right)
+        def _():
+            pltpu.make_async_copy(two, two, sem).wait()
+
+        @pl.when(has_left != has_right)
+        def _():
+            pltpu.make_async_copy(one, one, sem).wait()
+
+    def grad_copy(t, c, side, other):
         return pltpu.make_async_remote_copy(
-            src_ref=halo_out.at[side, t, c], dst_ref=pool.at[t, c, pl.ds(start, PATCH), :],
-            send_sem=halo_send.at[side], recv_sem=halo_recv.at[t, c, side],
+            src_ref=grad_out.at[side, t, c], dst_ref=grad_in.at[t, c, 1 - side],
+            send_sem=grad_send, recv_sem=grad_recv.at[t, c],
             device_id={"node": other}, device_id_type=MESH,
         )
 
-    def grad_copy(t, c, side, other, arrived=False):
-        far = side if arrived else 1 - side
-        return pltpu.make_async_remote_copy(
-            src_ref=grad_out.at[side, t, c], dst_ref=grad_in.at[t, c, far],
-            send_sem=grad_send.at[side], recv_sem=grad_recv.at[t, c, far],
-            device_id={"node": other}, device_id_type=MESH,
-        )
-
-    outs = (att_hbm, dq_hbm, dk_hbm, dv_hbm)
+    outs = [landed.at[t] for t in range(4)]
 
     def out_copy(t, c, d):
         peer = peers[d]
@@ -229,10 +229,8 @@
         return jnp.concatenate([pool[t, c, :PATCH], pool[t, c, PATCH + own:]], 0)
 
     def halo_wait(t, c):
-        for side, other, there in sides:
-            @pl.when(there)
-            def _():
-                halo_arrived(t, c, side, other).wait_recv()
+        block = pool.at[t, c]
+        sides_wait(block.at[pl.ds(0, 2 * PATCH)], block.at[pl.ds(0, PATCH)], halo_recv.at[t, c])
 
     def send_grad(t, c, grad):
         for side, other, there in sides:
@@ -273,7 +271,7 @@
             dot(turned[3, c, low:high], kept[0, c * group + h]) + dot(far_values_t[low:high], probs[h][2])
             for h, (low, high) in enumerate(span)
         ]
-        result[0, c] = jnp.concatenate(mixed, 0).T.astype(BF16)
+        result[0, c] = jnp.concatenate(mixed, 0).astype(BF16).T
         out_start(0, c)
         in_wait(3, c)
         turned[1, c] = rows_in[1, c].T
@@ -300,7 +298,7 @@
                 (dot(turned[2, c, low:high], close_scores) + dot(far_keys_t[low:high], far_scores)) * SCALE
             )
         send_grad(0, c, dk * SCALE)
-        result[1, c] = jnp.concatenate(dq_all, 0).T.astype(BF16)
+        result[1, c] = jnp.concatenate(dq_all, 0).astype(BF16).T
         out_start(1, c)
 
     def finish(c):
@@ -314,10 +312,7 @@
             )
             if t == 0:
                 total = total * SCALE
-            for side, other, there in sides:
-                @pl.when(there)
-                def _():
-                    grad_copy(t, c, side, other, arrived=True).wait_recv()
+            sides_wait(grad_in.at[t, c], grad_in.at[t, c, 0], grad_recv.at[t, c])
             for o in range(patches):
                 rows = slice(o * PATCH, (o + 1) * PATCH)
                 block = total[rows]
@@ -342,23 +337,17 @@
 
     sent = result.at[:, :, pl.ds(0, own - part), :]
     pltpu.make_async_copy(sent, sent, in_send).wait()
-    for side, other, there in sides:
-        @pl.when(there)
-        def _():
-            for out, sem in ((halo_out, halo_send), (grad_out, grad_send)):
-                block = out.at[side]
-                pltpu.make_async_copy(block, block, sem.at[side]).wait()
+    sides_wait(halo_out, halo_out.at[0], halo_send)
+    sides_wait(grad_out, grad_out.at[0], grad_send)
     pltpu.make_async_copy(sent, sent, out_send).wait()
     pltpu.make_async_copy(result, result, out_recv).wait()
 
 
-def write_out(*refs):
-    sems = refs[8]
-    copies = [pltpu.make_async_copy(refs[i], refs[4 + i], sems.at[i]) for i in range(4)]
-    for copy in copies:
-        copy.start()
-    for copy in copies:
-        copy.wait()
+def write_out(landed, *refs):
+    *outs, sem = refs
+    for t, out in enumerate(outs):
+        pltpu.make_async_copy(landed.at[t], out, sem).start()
+    pltpu.make_async_copy(landed, landed, sem).wait()
 
 
 def solution(mesh):
@@ -373,9 +362,9 @@
         dma = pltpu.SemaphoreType.DMA
         landed = pl.pallas_call(
             functools.partial(kernel, heads, nodes),
-            out_shape=[pltpu.VMEM((part, model), BF16)] * 4,
+            out_shape=pltpu.VMEM((4, part, model), BF16),
             in_specs=[any_spec] * 5,
-            out_specs=[pl.BlockSpec(memory_space=pltpu.VMEM)] * 4,
+            out_specs=pl.BlockSpec(memory_space=pltpu.VMEM),
             scratch_shapes=[
                 pltpu.SMEM(neighbours.shape, jnp.int32),
                 dma,
@@ -391,10 +380,10 @@
                 pltpu.SemaphoreType.REGULAR,
                 dma,
                 dma((4, chunks)),
-                dma((2,)),
-                dma((2, chunks, 2)),
-                dma((2,)),
-                dma((2, chunks, 2)),
+                dma,
+                dma((2, chunks)),
+                dma,
+                dma((2, chunks)),
                 dma,
                 dma,
             ],
@@ -403,10 +392,10 @@
         return pl.pallas_call(
             write_out,
             out_shape=[jax.ShapeDtypeStruct((part, model), BF16)] * 4,
-            in_specs=[pl.BlockSpec(memory_space=pltpu.VMEM)] * 4,
+            in_specs=[pl.BlockSpec(memory_space=pltpu.VMEM)],
             out_specs=[any_spec] * 4,
-            scratch_shapes=[dma((4,))],
-        )(*[pltpu.with_memory_space_constraint(x, pltpu.VMEM) for x in landed])
+            scratch_shapes=[dma],
+        )(pltpu.with_memory_space_constraint(landed, pltpu.VMEM))
 
     rows = P(("grp", "node", "head"), None)
     return jax.shard_map(

time: 21.5 us -> 21.3 us (level)
  no operation moved by 1% of the time
where the time goes in v4:
time: 21.3 us; the launch traced here: 21.2 us
  Pallas kernels  20.5 us (96%)
  between operations  0.64 us (3%)
    pallas_call x1, Pallas kernels, shards(): pl.pallas_call(functools.partial(kernel, heads, nodes), out_shape=pltpu.V...  19.7 us
    pallas_call x1, Pallas kernels, shards(): pl.pallas_call(write_out, out_shape=[jax.ShapeDtypeStruct((part, model),...  0.79 us

profile of v4, /device:TPU:0, one launch (start us, length us, event | category | flops | bytes accessed | tf_op | source)
XLA Modules:
  0.0 21.2 jit_solution(5697974125756337610)
XLA Ops:
  0.6 19.7 %shard_map.84.landed = bf16[4,64,1024]{2,1,0:T(8,128)(2,1)S(1)} custom-call(s32[8,8]{1,0:T(8,128)} %nbr_hbm.1, bf16[64,1024]{1,0:T(8,128)(2,1)} %q_hbm.1, bf16[64,1024]{1,0:T(8,128)(2,1)} %k_hbm.1, bf16[64,1024]{1,0:T(8,128)(2,1)} %v_hbm.1, bf16[64,1024]{1,0:T(8,128)(2,1)} %g_hbm.1), custom_call_target="tpu_custom_call" | custom-call | tf_op jit(solution)/shard_map/pallas_call | solution.py:363
  20.4 0.8 %shard_map.85 = (bf16[64,1024]{1,0:T(8,128)(2,1)}, bf16[64,1024]{1,0:T(8,128)(2,1)}, bf16[64,1024]{1,0:T(8,128)(2,1)}, bf16[64,1024]{1,0:T(8,128)(2,1)}) custom-call(bf16[4,64,1024]{2,1,0:T(8,128)(2,1)S(1)} %shard_map.84.landed), custom_call_target="tpu_custom_call" | custom-call | tf_op jit(solution)/shard_map/pallas_call | solution.py:392
